TPU v7x, 32 devices: a whole 2x2x4 slice. The times are simulated.
32 devices in a mesh: dp: 8 (over y, x, core), tensor: 4 (over z).
Axes of the slice: x: 2, y: 2, z: 4, core: 2. Of those that a mesh axis runs over, the one named last changes fastest.
Arguments:
- tokens: bfloat16 [8192, 2048], P('dp'), may hold values from -6 to 6
- cotangent: bfloat16 [8192, 2048], P('dp'), may hold values from -6 to 6
- segment_ids: int32 [8, 1024], P('dp'), may hold values from 0 to 2, never falling along the last dimension, each value on 1 to 768 neighbouring positions
- step_count: int32 [1], replicated, may hold values from 2 to 4
- norm_gains: float32 [2, 2048], P(None, 'dp'), may hold values from 0.5 to 1.5
- gains_first: float32 [2, 2048], P(None, 'dp'), may hold values from -0.0004272461 to 0.0004272461
- gains_second: float32 [2, 2048], P(None, 'dp'), may hold values from 9.5358565e-09 to 1.5211961e-07
- w_query: float32 [2048, 2048], P('dp', 'tensor'), may hold values from -0.125 to 0.125
- query_first: float32 [2048, 2048], P('dp', 'tensor'), may hold values from -0.00015258789 to 0.00015258789
- query_second: float32 [2048, 2048], P('dp', 'tensor'), may hold values from 1.4757873e-09 to 2.3839641e-08
- w_keyval: float32 [2, 2048, 256], P(None, 'dp', 'tensor'), may hold values from -0.125 to 0.125
- keyval_first: float32 [2, 2048, 256], P(None, 'dp', 'tensor'), may hold values from -0.0004272461 to 0.0004272461
- keyval_second: float32 [2, 2048, 256], P(None, 'dp', 'tensor'), may hold values from 1.0353215e-08 to 1.6710453e-07
- w_out: float32 [2048, 2048], P('tensor', 'dp'), may hold values from -1.5 to 1.5
- out_first: float32 [2048, 2048], P('tensor', 'dp'), may hold values from -1.5258789e-05 to 1.5258789e-05
- out_second: float32 [2048, 2048], P('tensor', 'dp'), may hold values from 1.7709447e-11 to 2.860757e-10
- w_gateup: float32 [2, 2048, 5632], P(None, 'dp', 'tensor'), may hold values from -0.125 to 0.125
- gateup_first: float32 [2, 2048, 5632], P(None, 'dp', 'tensor'), may hold values from -5.340576e-05 to 5.340576e-05
- gateup_second: float32 [2, 2048, 5632], P(None, 'dp', 'tensor'), may hold values from 1.4757873e-10 to 2.3839641e-09
- w_down: float32 [5632, 2048], P('tensor', 'dp'), may hold values from -0.15625 to 0.15625
- down_first: float32 [5632, 2048], P('tensor', 'dp'), may hold values from -4.5776367e-05 to 4.5776367e-05
- down_second: float32 [5632, 2048], P('tensor', 'dp'), may hold values from 1.1806298e-10 to 1.9071713e-09
Outputs:
- layer_out: bfloat16 [8192, 2048], P('dp')
- input_grad: float32 [8192, 2048], P('dp')
- grad_norm: float32 [1], replicated
- gains_moment: float32 [2, 2048], P(None, 'dp')
- gains_square: float32 [2, 2048], P(None, 'dp')
- gains_new: float32 [2, 2048], P(None, 'dp')
- query_moment: float32 [2048, 2048], P('dp', 'tensor')
- query_square: float32 [2048, 2048], P('dp', 'tensor')
- query_new: float32 [2048, 2048], P('dp', 'tensor')
- keyval_moment: float32 [2, 2048, 256], P(None, 'dp', 'tensor')
- keyval_square: float32 [2, 2048, 256], P(None, 'dp', 'tensor')
- keyval_new: float32 [2, 2048, 256], P(None, 'dp', 'tensor')
- out_moment: float32 [2048, 2048], P('tensor', 'dp')
- out_square: float32 [2048, 2048], P('tensor', 'dp')
- out_new: float32 [2048, 2048], P('tensor', 'dp')
- gateup_moment: float32 [2, 2048, 5632], P(None, 'dp', 'tensor')
- gateup_square: float32 [2, 2048, 5632], P(None, 'dp', 'tensor')
- gateup_new: float32 [2, 2048, 5632], P(None, 'dp', 'tensor')
- down_moment: float32 [5632, 2048], P('tensor', 'dp')
- down_square: float32 [5632, 2048], P('tensor', 'dp')
- down_new: float32 [5632, 2048], P('tensor', 'dp')
Inputs may be any that keep to these rules, and one draw needn't show every extreme that they name: `segment_ids`: in each batch row the segment ids never fall, all 3 ids occur, and the longest sequence of a row has 768 tokens; a token attends to the earlier tokens of its own sequence only.
All inputs are finite; a program needn't handle non-finite values.
Results may differ from a plain program's by a relative error of at most 0.017.
Values may be sent and summed in bfloat16 or wider, within the bound.
A program may use at most 320 MiB of HBM per device.

v0:
```python
import jax
import jax.numpy as jnp
from jax import lax
from jax.sharding import PartitionSpec as P

HD = 64
norm_eps = 1e-05
beta_first = 0.9
beta_second = 0.95
adam_eps = 1e-08
weight_decay = 0.1
weight_rate = 0.02
out_rate = 0.1
gain_rate = 0.2
clip_limit = 1.0
masked_value = -1000000000.0


def positions(segment):
    length = segment.shape[0]
    indices = jnp.arange(length, dtype=jnp.int32)
    earlier = jnp.concatenate([segment[:1] - 1, segment[:-1]])
    begins = jnp.where(segment != earlier, indices, jnp.zeros_like(indices))
    return indices - lax.cummax(begins, axis=0)


def rotary_tables(places, width):
    half_width = width // 2
    frequency = jnp.power(10000.0, -jnp.arange(half_width, dtype=jnp.float32) * (2.0 / width))
    angles = places.astype(jnp.float32)[:, None] * frequency[None, :]
    cosine_table = jnp.concatenate([jnp.cos(angles), jnp.cos(angles)], axis=-1)
    sine_table = jnp.concatenate([jnp.sin(angles), jnp.sin(angles)], axis=-1)
    return (cosine_table, sine_table)


def rotate(values, cosine_table, sine_table):
    half_width = values.shape[-1] // 2
    turned = jnp.concatenate([-values[..., half_width:], values[..., :half_width]], axis=-1)
    return values * cosine_table[:, None, :] + turned * sine_table[:, None, :]


def unrotate(gradient, cosine_table, sine_table):
    half_width = gradient.shape[-1] // 2
    along_sine = gradient * sine_table[:, None, :]
    turned = jnp.concatenate([along_sine[..., half_width:], -along_sine[..., :half_width]], axis=-1)
    return gradient * cosine_table[:, None, :] + turned


def over_rows(left, right):
    return lax.dot_general(
        left, right, (((0,), (0,)), ((), ())), preferred_element_type=jnp.float32
    )


def against(left, right):
    return lax.dot_general(
        left, right, (((1,), (1,)), ((), ())), preferred_element_type=jnp.float32
    )


def norm_back(grad_output, unit_rows, inverse, gain):
    scaled = grad_output * gain
    gain_grad = jnp.sum(grad_output * unit_rows, axis=0)
    inner_mean = jnp.mean(scaled * unit_rows, axis=-1, keepdims=True)
    return (inverse * (scaled - unit_rows * inner_mean), gain_grad)


def adam_step(weight, first, second, gradient, clip_factor, step_float, step_rate, decay_rate):
    gradient = gradient * clip_factor
    first = beta_first * first + (1.0 - beta_first) * gradient
    second = beta_second * second + (1.0 - beta_second) * gradient * gradient
    correct_one = 1.0 - jnp.power(beta_first, step_float)
    correct_two = 1.0 - jnp.power(beta_second, step_float)
    update = first / correct_one / (jnp.sqrt(second / correct_two) + adam_eps)
    return (first, second, weight - step_rate * (update + decay_rate * weight))


def on_device(
    tokens,
    cotangent,
    segment_ids,
    step_count,
    norm_gains,
    gains_first,
    gains_second,
    w_query,
    query_first,
    query_second,
    w_keyval,
    keyval_first,
    keyval_second,
    w_out,
    out_first,
    out_second,
    w_gateup,
    gateup_first,
    gateup_second,
    w_down,
    down_first,
    down_second,
):
    gathered = (
        lax.all_gather(norm_gains.astype(jnp.bfloat16), "dp", axis=1, tiled=True),
        lax.all_gather(w_query.astype(jnp.bfloat16), "dp", axis=0, tiled=True),
        lax.all_gather(w_keyval.astype(jnp.bfloat16), "dp", axis=1, tiled=True),
        lax.all_gather(w_out.astype(jnp.bfloat16), "dp", axis=1, tiled=True),
        lax.all_gather(w_gateup.astype(jnp.bfloat16), "dp", axis=1, tiled=True),
        lax.all_gather(w_down.astype(jnp.bfloat16), "dp", axis=1, tiled=True),
    )
    gain_rows, query_weight, keyval_weight, out_weight, gateup_weight, down_weight = gathered
    gain_values = gain_rows.astype(jnp.float32)
    length = tokens.shape[0]
    segment = segment_ids[0]
    local_heads = query_weight.shape[1] // HD
    local_groups = keyval_weight.shape[2] // HD
    group_size = local_heads // local_groups
    cosine_table, sine_table = rotary_tables(positions(segment), HD)
    indices = jnp.arange(length, dtype=jnp.int32)
    block_rows = min(512, length)
    starts = jnp.arange(length // block_rows, dtype=jnp.int32) * block_rows
    inverse_scale = HD ** (-0.5)
    values_in = tokens.astype(jnp.float32)
    inverse_one = lax.rsqrt(jnp.mean(values_in * values_in, axis=-1, keepdims=True) + norm_eps)
    unit_one = values_in * inverse_one
    normed_one = (unit_one * gain_values[0]).astype(jnp.bfloat16)
    query_raw = jnp.dot(normed_one, query_weight, preferred_element_type=jnp.float32)
    queries = rotate(query_raw.reshape(length, local_heads, HD), cosine_table, sine_table).astype(
        jnp.bfloat16
    )
    queries = queries.reshape(length, local_groups, group_size, HD)
    keyval_raw = jnp.einsum(
        "nd,sdk->snk", normed_one, keyval_weight, preferred_element_type=jnp.float32
    )
    key_rows = rotate(
        keyval_raw[0].reshape(length, local_groups, HD), cosine_table, sine_table
    ).astype(jnp.bfloat16)
    value_rows = keyval_raw[1].reshape(length, local_groups, HD).astype(jnp.bfloat16)

    def block_scores(start):
        query_block = lax.dynamic_slice_in_dim(queries, start, block_rows, 0)
        segment_block = lax.dynamic_slice_in_dim(segment, start, block_rows, 0)
        row_index = start + jnp.arange(block_rows, dtype=jnp.int32)
        allowed = (segment_block[:, None] == segment[None, :]) & (
            row_index[:, None] >= indices[None, :]
        )
        raw_scores = jnp.einsum(
            "qkgh,pkh->kgqp", query_block, key_rows, preferred_element_type=jnp.float32
        )
        return (query_block, jnp.where(allowed, raw_scores * inverse_scale, masked_value))

    def forward_block(start):
        query_block, scaled = block_scores(start)
        highest = jnp.max(scaled, axis=-1, keepdims=True)
        lifted = jnp.exp(scaled - highest)
        row_total = jnp.sum(lifted, axis=-1, keepdims=True)
        soft_weights = (lifted / row_total).astype(jnp.bfloat16)
        mixed = jnp.einsum(
            "kgqp,pkh->qkgh", soft_weights, value_rows, preferred_element_type=jnp.float32
        )
        return (
            mixed.astype(jnp.bfloat16).reshape(block_rows, local_heads * HD),
            (highest + jnp.log(row_total))[..., 0],
        )

    mixed_blocks, logsum_blocks = lax.map(forward_block, starts)
    mixture = mixed_blocks.reshape(length, local_heads * HD)
    branch_partial = jnp.dot(mixture, out_weight, preferred_element_type=jnp.float32)
    branch = lax.psum(branch_partial, "tensor")
    middle = values_in + branch
    inverse_two = lax.rsqrt(jnp.mean(middle * middle, axis=-1, keepdims=True) + norm_eps)
    unit_two = middle * inverse_two
    normed_two = (unit_two * gain_values[1]).astype(jnp.bfloat16)
    gateup = jnp.einsum(
        "nd,sdf->snf", normed_two, gateup_weight, preferred_element_type=jnp.float32
    )
    hidden = (jax.nn.silu(gateup[0]) * gateup[1]).astype(jnp.bfloat16)
    feed_out = lax.psum(
        jnp.dot(hidden, down_weight, preferred_element_type=jnp.float32).astype(jnp.bfloat16),
        "tensor",
    ).astype(jnp.float32)
    layer_out = (middle + feed_out).astype(jnp.bfloat16)
    regathered = (
        lax.all_gather(norm_gains.astype(jnp.bfloat16), "dp", axis=1, tiled=True),
        lax.all_gather(w_query.astype(jnp.bfloat16), "dp", axis=0, tiled=True),
        lax.all_gather(w_keyval.astype(jnp.bfloat16), "dp", axis=1, tiled=True),
        lax.all_gather(w_out.astype(jnp.bfloat16), "dp", axis=1, tiled=True),
        lax.all_gather(w_gateup.astype(jnp.bfloat16), "dp", axis=1, tiled=True),
        lax.all_gather(w_down.astype(jnp.bfloat16), "dp", axis=1, tiled=True),
    )
    gain_rows, query_weight, keyval_weight, out_weight, gateup_weight, down_weight = regathered
    gain_values = gain_rows.astype(jnp.float32)
    grad_down_weight = over_rows(hidden, cotangent)
    grad_hidden = against(cotangent, down_weight)
    gate_values = gateup[0]
    up_values = gateup[1]
    sigmoid_gate = jax.nn.sigmoid(gate_values)
    grad_gate = grad_hidden * up_values * sigmoid_gate * (1.0 + gate_values * (1.0 - sigmoid_gate))
    grad_up = grad_hidden * gate_values * sigmoid_gate
    grad_gateup = jnp.stack([grad_gate, grad_up]).astype(jnp.bfloat16)
    grad_gateup_weight = jnp.einsum(
        "nd,snf->sdf", normed_two, grad_gateup, preferred_element_type=jnp.float32
    )
    partial_two = jnp.einsum(
        "snf,sdf->nd", grad_gateup, gateup_weight, preferred_element_type=jnp.float32
    )
    grad_normed_two = lax.psum(partial_two, "tensor")
    grad_from_two, gain_grad_two = norm_back(grad_normed_two, unit_two, inverse_two, gain_values[1])
    grad_middle = cotangent.astype(jnp.float32) + grad_from_two
    grad_branch = grad_middle.astype(jnp.bfloat16)
    grad_out_weight = over_rows(mixture, grad_branch)
    grad_mixture = (
        against(grad_branch, out_weight)
        .astype(jnp.bfloat16)
        .reshape(length, local_groups, group_size, HD)
    )

    def backward_block(carried, pieces):
        start, logsum = pieces
        query_block, scaled = block_scores(start)
        soft_weights = jnp.exp(scaled - logsum[..., None])
        grad_block = lax.dynamic_slice_in_dim(grad_mixture, start, block_rows, 0)
        grad_soft = jnp.einsum(
            "qkgh,pkh->kgqp", grad_block, value_rows, preferred_element_type=jnp.float32
        )
        spread = jnp.sum(soft_weights * grad_soft, axis=-1, keepdims=True)
        grad_scores = (soft_weights * (grad_soft - spread) * inverse_scale).astype(jnp.bfloat16)
        grad_query = jnp.einsum(
            "kgqp,pkh->qkgh", grad_scores, key_rows, preferred_element_type=jnp.float32
        )
        grad_key = carried[0] + jnp.einsum(
            "kgqp,qkgh->pkh", grad_scores, query_block, preferred_element_type=jnp.float32
        )
        grad_value = carried[1] + jnp.einsum(
            "kgqp,qkgh->pkh",
            soft_weights.astype(jnp.bfloat16),
            grad_block,
            preferred_element_type=jnp.float32,
        )
        return ((grad_key, grad_value), grad_query)

    zero_rows = jnp.zeros((length, local_groups, HD), jnp.float32)
    (grad_keys, grad_values), grad_queries = lax.scan(
        backward_block, (zero_rows, zero_rows), (starts, logsum_blocks)
    )
    grad_queries = grad_queries.reshape(length, local_heads, HD)
    grad_query_raw = (
        unrotate(grad_queries, cosine_table, sine_table)
        .astype(jnp.bfloat16)
        .reshape(length, local_heads * HD)
    )
    grad_key_raw = unrotate(grad_keys, cosine_table, sine_table).reshape(length, local_groups * HD)
    grad_keyval = jnp.stack([grad_key_raw, grad_values.reshape(length, local_groups * HD)]).astype(
        jnp.bfloat16
    )
    grad_query_weight = over_rows(normed_one, grad_query_raw)
    grad_keyval_weight = jnp.einsum(
        "nd,snk->sdk", normed_one, grad_keyval, preferred_element_type=jnp.float32
    )
    partial_one = against(grad_query_raw, query_weight) + jnp.einsum(
        "snk,sdk->nd", grad_keyval, keyval_weight, preferred_element_type=jnp.float32
    )
    grad_normed_one = lax.psum(partial_one.astype(jnp.bfloat16), "tensor").astype(jnp.float32)
    grad_from_one, gain_grad_one = norm_back(grad_normed_one, unit_one, inverse_one, gain_values[0])
    input_grad = grad_middle + grad_from_one
    gain_grads = jnp.stack([gain_grad_one, gain_grad_two])
    reduced = (
        lax.psum_scatter(gain_grads, "dp", scatter_dimension=1, tiled=True),
        lax.psum_scatter(grad_query_weight, "dp", scatter_dimension=0, tiled=True),
        lax.psum_scatter(grad_keyval_weight, "dp", scatter_dimension=1, tiled=True),
        lax.psum_scatter(grad_out_weight, "dp", scatter_dimension=1, tiled=True),
        lax.psum_scatter(grad_gateup_weight, "dp", scatter_dimension=1, tiled=True),
        lax.psum_scatter(grad_down_weight, "dp", scatter_dimension=1, tiled=True),
    )
    first_owner = (lax.axis_index("tensor") == 0).astype(jnp.float32)
    local_square = first_owner * jnp.sum(reduced[0] * reduced[0]) + sum(
        (jnp.sum(g * g) for g in reduced[1:])
    )
    square_total = lax.psum(local_square, ("dp", "tensor"))
    grad_norm = jnp.sqrt(square_total)
    clip_factor = jnp.minimum(1.0, clip_limit / (grad_norm + 1e-06))
    step_float = step_count[0].astype(jnp.float32)
    params = (norm_gains, w_query, w_keyval, w_out, w_gateup, w_down)
    states = (
        (gains_first, gains_second),
        (query_first, query_second),
        (keyval_first, keyval_second),
        (out_first, out_second),
        (gateup_first, gateup_second),
        (down_first, down_second),
    )
    step_rates = (gain_rate, weight_rate, weight_rate, out_rate, weight_rate, weight_rate)
    decay_rates = (0.0, weight_decay, weight_decay, weight_decay, weight_decay, weight_decay)
    results = []
    for position_index in range(6):
        first, second = states[position_index]
        results.extend(
            adam_step(
                params[position_index],
                first,
                second,
                reduced[position_index],
                clip_factor,
                step_float,
                step_rates[position_index],
                decay_rates[position_index],
            )
        )
    return (
        layer_out,
        input_grad,
        grad_norm.reshape(1),
        results[0],
        results[1],
        results[2],
        results[3],
        results[4],
        results[5],
        results[6],
        results[7],
        results[8],
        results[9],
        results[10],
        results[11],
        results[12],
        results[13],
        results[14],
        results[15],
        results[16],
        results[17],
    )


def solution(mesh):
    in_specs = (
        P("dp", None),
        P("dp", None),
        P("dp", None),
        P(),
        P(None, "dp"),
        P(None, "dp"),
        P(None, "dp"),
        P("dp", "tensor"),
        P("dp", "tensor"),
        P("dp", "tensor"),
        P(None, "dp", "tensor"),
        P(None, "dp", "tensor"),
        P(None, "dp", "tensor"),
        P("tensor", "dp"),
        P("tensor", "dp"),
        P("tensor", "dp"),
        P(None, "dp", "tensor"),
        P(None, "dp", "tensor"),
        P(None, "dp", "tensor"),
        P("tensor", "dp"),
        P("tensor", "dp"),
        P("tensor", "dp"),
    )
    out_specs = (
        P("dp", None),
        P("dp", None),
        P(),
        P(None, "dp"),
        P(None, "dp"),
        P(None, "dp"),
        P("dp", "tensor"),
        P("dp", "tensor"),
        P("dp", "tensor"),
        P(None, "dp", "tensor"),
        P(None, "dp", "tensor"),
        P(None, "dp", "tensor"),
        P("tensor", "dp"),
        P("tensor", "dp"),
        P("tensor", "dp"),
        P(None, "dp", "tensor"),
        P(None, "dp", "tensor"),
        P(None, "dp", "tensor"),
        P("tensor", "dp"),
        P("tensor", "dp"),
        P("tensor", "dp"),
    )
    return jax.shard_map(
        on_device, mesh=mesh, in_specs=in_specs, out_specs=out_specs, check_vma=False
    )
```

profile of v0, /device:TPU:0, one launch (start us, length us, event | category | flops | bytes accessed | tf_op | source)
XLA Modules:
  0.0 1800.6 jit_solution(3728736641630619204)
XLA Ops:
  26.0 14.2 all_gather.26
  51.2 37.7 %while.28 = (s32[]{:T(128)}, bf16[2,512,512]{2,1,0:T(8,128)(2,1)}, f32[2,1,8,512]{3,2,1,0:T(8,128)}, s32[2]{0:T(128)S(1)}, s32[1024]{0:T(1024)S(1)}, /*index=5*/...) while((s32[]{:T(128)}, bf16[2,512,512]{2,1,0:T(8,128)(2,1)}, ...), condition=%wide.region_6.7_spmd.clone, body=%wide.region_3.6_spmd.clone.sunk | while | flops 1125904896 | bytes 64371432 | solution.py:165
  100.9 287.2 %all-reduce.5.cloned.1.call-done = f32[1024,2048]{1,0:T(8,128)} async-done(((f32[1024,2048]{1,0:T(8,128)}), f32[1024,2048]{1,0:T(8,128)}) %all-reduce.5.cloned.1.call-update) | async-done | bytes 8388624 | tf_op jit(solution)/shard_map/psum | solution.py:168
  397.4 59.8 %all-gather.9.cloned.1.call-done = bf16[2,2048,1408]{2,1,0:T(8,128)(2,1)} async-done(((bf16[2,256,1408]{2,1,0:T(8,128)(2,1)}), bf16[2,2048,1408]{2,1,0:T(8,128)(2,1)}) %all-gather.9.cloned.1.call-update) | async-done | bytes 11534352 | tf_op jit(solution)/shard_map/all_gather | solution.py:107
  457.2 20.2 %convolution_bitcast_fusion.3 = f32[2,1024,1408]{2,1,0:T(8,128)} fusion(bf16[2,2048,1408]{2,1,0:T(8,128)(2,1)} %all-gather.9.cloned.1.call-done, f32[1024,2048]{1,0:T(8,128)} %get-tuple-element.339, f32[2048]{0:T(1024)S(1)} %bitcast.364, f32[1024]{0:T(1024)S(1)} %add_rsqrt_fusion), kind=kOutput, calls=%fused_computation.85 | convolution fusion | flops 11817451520 | bytes 31469568 | tf_op jit(solution)/shard_map/nd,sdf->snf/dot_general | solution.py:173
  477.4 26.5 %all-gather.11.cloned.1.call-done = bf16[1408,2048]{1,0:T(8,128)(2,1)} async-done(((bf16[1408,256]{1,0:T(8,128)(2,1)}), bf16[1408,2048]{1,0:T(8,128)(2,1)}) %all-gather.11.cloned.1.call-update) | async-done | bytes 5767184 | tf_op jit(solution)/shard_map/all_gather | solution.py:108
  503.9 15.6 fusion.71
  522.0 17.0 convolution_bitcast_fusion.4
  539.1 11.3 convolution_convert_fusion
  550.4 279.6 %all-reduce.7.cloned.1.call-done = f32[1024,2048]{1,0:T(8,128)} async-done(((f32[1024,2048]{1,0:T(8,128)}), f32[1024,2048]{1,0:T(8,128)}) %all-reduce.7.cloned.1.call-update) | async-done | bytes 8388624 | tf_op jit(solution)/shard_map/psum | solution.py:206
  850.9 129.5 %while.29 = (s32[]{:T(128)}, f32[1024,1,64]{0,2,1:T(8,128)}, f32[1024,1,64]{0,2,1:T(8,128)}, f32[2,512,1,8,64]{1,0,4,3,2:T(2,128)}, s32[2]{0:T(128)S(1)}, /*inde...) while((s32[]{:T(128)}, f32[1024,1,64]{0,2,1:T(8,128)}, ...), condition=%wide.region_14.15_spmd.clone, body=%wide.region_12.14_spmd.clone.sunk | while | flops 2728129024 | bytes 178878960 | solution.py:242
  859.7 10.8 fusion.181
  882.7 19.5 %dynamic_update_slice.22 = f32[2,512,1,8,64]{1,0,4,3,2:T(2,128)} dynamic-update-slice(f32[2,512,1,8,64]{1,0,4,3,2:T(2,128)} %get-tuple-element.553, f32[1,512,1,8,64]{1,0,4,3,2:T(1,128)S(1)} %copy.99, s32[]{:T(128)} %get-tuple-element.550, s32[]{:T(128)} %constant.54.clone.1..sunk.1, s32[]{:T(128)} %constant.54.clone.1..sunk.1, s32[]{:T(128)} %constant.54.clone.1..sunk.1, s32[]{:T(128)} %constant.54.clone.1..sunk.1) | dynamic-update-slice | bytes 2097156 | tf_op jit(solution)/shard_map/while/body/jit(dynamic_update_index_in_dim)/dynamic_update_slice | solution.py:242
  924.4 10.8 fusion.181
  947.4 19.5 %dynamic_update_slice.22 = f32[2,512,1,8,64]{1,0,4,3,2:T(2,128)} dynamic-update-slice(f32[2,512,1,8,64]{1,0,4,3,2:T(2,128)} %get-tuple-element.553, f32[1,512,1,8,64]{1,0,4,3,2:T(1,128)S(1)} %copy.99, s32[]{:T(128)} %get-tuple-element.550, s32[]{:T(128)} %constant.54.clone.1..sunk.1, s32[]{:T(128)} %constant.54.clone.1..sunk.1, s32[]{:T(128)} %constant.54.clone.1..sunk.1, s32[]{:T(128)} %constant.54.clone.1..sunk.1) | dynamic-update-slice | bytes 2097156 | tf_op jit(solution)/shard_map/while/body/jit(dynamic_update_index_in_dim)/dynamic_update_slice | solution.py:242
  1016.5 269.4 %all-reduce.9.cloned.1.call-done = (bf16[1024,2048]{1,0:T(8,128)(2,1)}, bf16[1024,2048]{1,0:T(8,128)(2,1)}) async-done(((bf16[1024,2048]{1,0:T(8,128)(2,1)}, bf16[1024,2048]{1,0:T(8,128)(2,1)}), (bf16[1024,2048]{1,0:T(8,128)(2,1)}, bf16[1024,2048]{1,0:T(8,128)(2,1)})) %all-reduce.9.cloned.1.call-update) | async-done | bytes 8388624 | tf_op jit(solution)/shard_map/psum | solution.py:177
  1292.4 11.3 fusion.124
  1304.4 21.0 %convolution_bitcast_fusion.2 = f32[2,2048,1408]{1,2,0:T(8,128)} fusion(bf16[1,1024,1408]{2,1,0:T(8,128)(2,1)} %copy-done.62, bf16[1,1024,1408]{2,1,0:T(8,128)(2,1)} %copy-done.61, f32[1024,2048]{1,0:T(8,128)} %get-tuple-element.339, f32[2048]{0:T(1024)S(1)} %bitcast.367, f32[1024]{0:T(1024)S(1)} %copy-done.52), kind=kOutput, calls=%fused_computation.61 | convolution fusion | flops 11820335104 | bytes 37236736 | tf_op jit(solution)/shard_map/nd,snf->sdf/dot_general | solution.py:200
  1337.5 42.0 %reduce-scatter.9.cloned.1.call-done = f32[256,512]{1,0:T(8,128)} async-done(((f32[2048,512]{1,0:T(8,128)}), f32[256,512]{1,0:T(8,128)}) %reduce-scatter.9.cloned.1.call-update) | async-done | bytes 524304 | tf_op jit(solution)/shard_map/reduce_scatter | solution.py:268
  1382.5 51.9 %reduce-scatter.13.cloned.1.call-done = f32[512,256]{1,0:T(8,128)} async-done(((f32[512,2048]{1,0:T(8,128)}), f32[512,256]{1,0:T(8,128)}) %reduce-scatter.13.cloned.1.call-update) | async-done | bytes 524304 | tf_op jit(solution)/shard_map/reduce_scatter | solution.py:270
  1446.3 27.9 %reduce-scatter.19.cloned.1.call-done = f32[256,2]{1,0:T(8,128)} async-done(((f32[2048,2]{1,0:T(8,128)}), f32[256,2]{1,0:T(8,128)}) %reduce-scatter.19.cloned.1.call-update) | async-done | bytes 2064
  1476.4 87.9 %reduce-scatter.17.cloned.1.call-done = f32[1408,256]{1,0:T(8,128)} async-done(((f32[1408,2048]{1,0:T(8,128)}), f32[1408,256]{1,0:T(8,128)}) %reduce-scatter.17.cloned.1.call-update) | async-done | bytes 1441808 | tf_op jit(solution)/shard_map/reduce_scatter | solution.py:272
  1566.7 147.2 %reduce-scatter.15.cloned.1.call-done = f32[2,256,1408]{1,2,0:T(8,128)} async-done(((f32[2,2048,1408]{1,2,0:T(8,128)}), f32[2,256,1408]{1,2,0:T(8,128)}) %reduce-scatter.15.cloned.1.call-update) | async-done | bytes 2883600 | tf_op jit(solution)/shard_map/reduce_scatter | solution.py:271
  1726.8 39.5 %psum.39 = f32[]{:T(128)} all-reduce(f32[]{:T(128)S(6)} %add.273), channel_id=1, replica_groups=mesh['dp'=8,'tensor'=4] {'dp','tensor'}, use_global_device_ids=true, to_apply=%region_31.32 | all-reduce | flops 1 | bytes 8 | tf_op jit(solution)/shard_map/psum | solution.py:278
  (300 shorter events, 279.5 us)
Async XLA Ops:
  7.2 18.8 %copy-start.37 = (f32[2,256,64]{1,2,0:T(8,128)S(1)}, f32[2,256,64]{1,2,0:T(8,128)}, u32[]{:S(2)}) copy-start(f32[2,256,64]{1,2,0:T(8,128)} %param.36) | copy-start | bytes 393220
  7.2 37.9 %all-gather.5.cloned.1.call-start = ((), (), s32[]{:S(2)}) async-start(), calls=%async_computation.6 | async-start | bytes 2359296 | tf_op jit(solution)/shard_map/all_gather | solution.py:104
  9.1 79.8 %all-gather.7.cloned.1.call-start = ((), (), s32[]{:S(2)}) async-start(), calls=%async_computation.7 | async-start | bytes 2359296 | tf_op jit(solution)/shard_map/all_gather | solution.py:106
  10.9 377.2 %all-reduce.5.cloned.1.call-start = ((), (), s32[]{:S(2)}) async-start(), calls=%async_computation.8 | async-start | bytes 16777216 | tf_op jit(solution)/shard_map/psum | solution.py:168
  11.0 29.3 %copy-start.2 = (bf16[1024,2048]{1,0:T(8,128)(2,1)S(1)}, bf16[1024,2048]{1,0:T(8,128)(2,1)}, u32[]{:S(2)}) copy-start(bf16[1024,2048]{1,0:T(8,128)(2,1)} %param.26) | copy-start | bytes 12582916
  22.9 22.1 %copy-start.47 = (f32[1,2048]{1,0:T(1,128)}, f32[1,2048]{1,0:T(1,128)S(1)}, u32[]{:S(2)}) copy-start(f32[1,2048]{1,0:T(1,128)S(1)} %get-tuple-element.356) | copy-start | bytes 24580
  26.0 19.0 %copy-start.53 = (f32[1024]{0:T(1024)}, f32[1024]{0:T(1024)S(1)}, u32[]{:S(2)}) copy-start(f32[1024]{0:T(1024)S(1)} %add_rsqrt_fusion.1) | copy-start | bytes 12292
  96.6 360.6 %all-gather.9.cloned.1.call-start = ((), (), s32[]{:S(2)}) async-start(), calls=%async_computation.9 | async-start | bytes 12976128 | tf_op jit(solution)/shard_map/all_gather | solution.py:107
  99.9 404.0 %all-gather.11.cloned.1.call-start = ((), (), s32[]{:S(2)}) async-start(), calls=%async_computation.10 | async-start | bytes 6488064 | tf_op jit(solution)/shard_map/all_gather | solution.py:108
  100.9 356.3 %copy-start.49 = (f32[1,2048]{1,0:T(1,128)S(1)}, f32[1,2048]{1,0:T(1,128)}, u32[]{:S(2)}) copy-start(f32[1,2048]{1,0:T(1,128)} %get-tuple-element.355) | copy-start | bytes 24580
  100.9 729.1 %all-reduce.7.cloned.1.call-start = ((), (), s32[]{:S(2)}) async-start(), calls=%async_computation.11 | async-start | bytes 16777216 | tf_op jit(solution)/shard_map/psum | solution.py:206
  397.4 440.3 %copy-start.51 = (f32[1024]{0:T(1024)}, f32[1024]{0:T(1024)S(1)}, u32[]{:S(2)}) copy-start(f32[1024]{0:T(1024)S(1)} %add_rsqrt_fusion) | copy-start | bytes 12292
  539.1 746.9 %all-reduce.9.cloned.1.call-start = ((), (), s32[]{:S(2)}) async-start(), calls=%async_computation.18 | async-start | bytes 16777216 | tf_op jit(solution)/shard_map/psum | solution.py:177
  830.0 9.4 copy-start.18
  881.6 20.6 %copy-start.7 = (f32[1024,1,64]{0,2,1:T(8,128)S(1)}, f32[1024,1,64]{0,2,1:T(8,128)}, u32[]{:S(2)}) copy-start(f32[1024,1,64]{0,2,1:T(8,128)} %get-tuple-element.551) | copy-start | bytes 786436 | tf_op jit(solution)/shard_map/while
  946.3 20.6 %copy-start.7 = (f32[1024,1,64]{0,2,1:T(8,128)S(1)}, f32[1024,1,64]{0,2,1:T(8,128)}, u32[]{:S(2)}) copy-start(f32[1024,1,64]{0,2,1:T(8,128)} %get-tuple-element.551) | copy-start | bytes 786436 | tf_op jit(solution)/shard_map/while
  972.1 8.3 copy-start.4
  995.2 340.7 %reduce-scatter.11.cloned.1.call-start = ((), (), s32[]{:S(2)}) async-start(), calls=%async_computation.13 | async-start | bytes 1179648 | tf_op jit(solution)/shard_map/reduce_scatter | solution.py:269
  1000.5 379.0 %reduce-scatter.9.cloned.1.call-start = ((), (), s32[]{:S(2)}) async-start(), calls=%async_computation.12 | async-start | bytes 4718592 | tf_op jit(solution)/shard_map/reduce_scatter | solution.py:268
  1007.4 427.0 %reduce-scatter.13.cloned.1.call-start = ((), (), s32[]{:S(2)}) async-start(), calls=%async_computation.14 | async-start | bytes 4718592 | tf_op jit(solution)/shard_map/reduce_scatter | solution.py:270
  1016.5 457.7 %reduce-scatter.19.cloned.1.call-start = ((), (), s32[]{:S(2)}) async-start(), calls=%async_computation.17 | async-start | bytes 1179648
  1292.3 272.0 %reduce-scatter.17.cloned.1.call-start = ((), (), s32[]{:S(2)}) async-start(), calls=%async_computation.16 | async-start | bytes 12976128 | tf_op jit(solution)/shard_map/reduce_scatter | solution.py:272
  1303.8 410.1 %reduce-scatter.15.cloned.1.call-start = ((), (), s32[]{:S(2)}) async-start(), calls=%async_computation.15 | async-start | bytes 25952256 | tf_op jit(solution)/shard_map/reduce_scatter | solution.py:271
  1718.4 48.7 %copy-start.10 = (f32[2,256,1408]{1,2,0:T(8,128)S(1)}, f32[2,256,1408]{1,2,0:T(8,128)}, u32[]{:S(2)}) copy-start(f32[2,256,1408]{1,2,0:T(8,128)} %reduce-scatter.15.cloned.1.call-done) | copy-start | bytes 8650756
  (63 other events, 240.4 us)
Sparse Core Ops, SparseCore 0:
  10.5 32.9 all-gather.4
  45.9 28.5 all-gather.6
  96.7 291.3 all-reduce.4
  390.5 66.6 all-gather.8
  459.5 44.3 all-gather.10
  539.2 290.8 all-reduce.6
  995.4 290.5 all-reduce.8
  1289.7 35.0 reduce-scatter.10
  1328.1 51.2 reduce-scatter.8
  1383.0 51.3 reduce-scatter.12
  1438.2 35.9 reduce-scatter.18
  1477.5 86.7 reduce-scatter.16
  1568.0 145.8 reduce-scatter.14
where the time goes:
time: 1810 us; the launch traced here: 1800 us
  waiting for transfers between devices  1280 us (71%)
  matrix products  218 us (12%)
  other arithmetic  120 us (7%)
  local copies, waits for them, and re-layouts  87.9 us (5%)
  blocking collectives  64.2 us (4%)
  between operations  22.3 us (1%)
    psum x1, waiting for transfers between devices, on_device(): branch = lax.psum(branch_partial, 'tensor')  287 us
    psum x1, waiting for transfers between devices, on_device(): grad_normed_two = lax.psum(partial_two, 'tensor')  280 us
    psum x1, waiting for transfers between devices, on_device(): lax.psum(jnp.dot(hidden, down_weight, preferred_element_type=jnp.float32)...  269 us
    reduce_scatter x1, waiting for transfers between devices, on_device(): lax.psum_scatter(grad_gateup_weight, 'dp', scatter_dimension=1, tiled=True)  147 us
    reduce_scatter x1, waiting for transfers between devices, on_device(): lax.psum_scatter(grad_down_weight, 'dp', scatter_dimension=1, tiled=True)  87.9 us
    all_gather x1, waiting for transfers between devices, on_device(): lax.all_gather(w_gateup.astype(jnp.bfloat16), 'dp', axis=1, tiled=True)  59.8 us
    reduce_scatter x1, waiting for transfers between devices, on_device(): lax.psum_scatter(grad_out_weight, 'dp', scatter_dimension=1, tiled=True)  51.9 us
    reduce_scatter x1, waiting for transfers between devices, on_device(): lax.psum_scatter(grad_query_weight, 'dp', scatter_dimension=0, tiled=True)  42 us
  transfers between devices with their start and end apart: 13, of which 10 were waited for; matrix products, arithmetic and copies ran while one was open for 10% of the time, Pallas kernels for 0%

commit v1 on v0

--- a/solution.py
+++ b/solution.py
@@ -275,7 +275,9 @@
     local_square = first_owner * jnp.sum(reduced[0] * reduced[0]) + sum(
         (jnp.sum(g * g) for g in reduced[1:])
     )
-    square_total = lax.psum(local_square, ("dp", "tensor"))
+    square_total = local_square
+    for kk in ("tensor", "dp"):
+        square_total = lax.psum(square_total, axis_name=kk)
     grad_norm = jnp.sqrt(square_total)
     clip_factor = jnp.minimum(1.0, clip_limit / (grad_norm + 1e-06))
     step_float = step_count[0].astype(jnp.float32)

time: 1810 us -> 1800 us (level)
    psum x1 -> x2, blocking collectives: 39.5 us -> 24.8 us  [on_device(): square_total = lax.psum(square_total, axis_name=kk)]
  transfers between devices with their start and end apart: 13 -> 13, of which waited for: 10 -> 10; matrix products, arithmetic and copies ran while one was open for 10% -> 9% of each run, Pallas kernels for 0% -> 0%
where the time goes in v1:
time: 1800 us; the launch traced here: 1790 us
  waiting for transfers between devices  1290 us (72%)
  matrix products  218 us (12%)
  other arithmetic  120 us (7%)
  local copies, waits for them, and re-layouts  85.7 us (5%)
  blocking collectives  49.5 us (3%)
  between operations  22.2 us (1%)
    psum x1, waiting for transfers between devices, on_device(): branch = lax.psum(branch_partial, 'tensor')  287 us
    psum x1, waiting for transfers between devices, on_device(): grad_normed_two = lax.psum(partial_two, 'tensor')  280 us
    psum x1, waiting for transfers between devices, on_device(): lax.psum(jnp.dot(hidden, down_weight, preferred_element_type=jnp.float32)...  269 us
    reduce_scatter x1, waiting for transfers between devices, on_device(): lax.psum_scatter(grad_gateup_weight, 'dp', scatter_dimension=1, tiled=True)  147 us
    reduce_scatter x1, waiting for transfers between devices, on_device(): lax.psum_scatter(grad_down_weight, 'dp', scatter_dimension=1, tiled=True)  87.9 us
    all_gather x1, waiting for transfers between devices, on_device(): lax.all_gather(w_gateup.astype(jnp.bfloat16), 'dp', axis=1, tiled=True)  59.8 us
    reduce_scatter x1, waiting for transfers between devices, on_device(): lax.psum_scatter(grad_out_weight, 'dp', scatter_dimension=1, tiled=True)  51.8 us
    reduce_scatter x1, waiting for transfers between devices, on_device(): lax.psum_scatter(grad_query_weight, 'dp', scatter_dimension=0, tiled=True)  41.6 us
  transfers between devices with their start and end apart: 13, of which 10 were waited for; matrix products, arithmetic and copies ran while one was open for 9% of the time, Pallas kernels for 0%

profile of v1, /device:TPU:0, one launch (start us, length us, event | category | flops | bytes accessed | tf_op | source)
XLA Modules:
  0.0 1793.7 jit_solution(14061763398037035738)
XLA Ops:
  26.0 14.2 all_gather.26
  51.2 35.8 %while.28 = (s32[]{:T(128)}, bf16[2,512,512]{2,1,0:T(8,128)(2,1)S(1)}, f32[2,1,8,512]{3,2,1,0:T(8,128)}, s32[2]{0:T(128)S(1)}, s32[1024]{0:T(1024)S(1)}, /*index...) while((s32[]{:T(128)}, ...), condition=%wide.region_6.7_spmd.clone, body=%wide.region_3.6_spmd.clone.sunk | while | flops 1125904896 | bytes 55982772 | solution.py:165
  99.1 287.1 %all-reduce.5.cloned.1.call-done = f32[1024,2048]{1,0:T(8,128)} async-done(((f32[1024,2048]{1,0:T(8,128)}), f32[1024,2048]{1,0:T(8,128)}) %all-reduce.5.cloned.1.call-update) | async-done | bytes 8388624 | tf_op jit(solution)/shard_map/psum | solution.py:168
  395.5 59.8 %all-gather.9.cloned.1.call-done = bf16[2,2048,1408]{2,1,0:T(8,128)(2,1)} async-done(((bf16[2,256,1408]{2,1,0:T(8,128)(2,1)}), bf16[2,2048,1408]{2,1,0:T(8,128)(2,1)}) %all-gather.9.cloned.1.call-update) | async-done | bytes 11534352 | tf_op jit(solution)/shard_map/all_gather | solution.py:107
  455.3 20.2 %convolution_bitcast_fusion.3 = f32[2,1024,1408]{2,1,0:T(8,128)} fusion(bf16[2,2048,1408]{2,1,0:T(8,128)(2,1)} %all-gather.9.cloned.1.call-done, f32[1024,2048]{1,0:T(8,128)} %get-tuple-element.339, f32[2048]{0:T(1024)S(1)} %bitcast.364, f32[1024]{0:T(1024)S(1)} %add_rsqrt_fusion), kind=kOutput, calls=%fused_computation.85 | convolution fusion | flops 11817451520 | bytes 31469568 | tf_op jit(solution)/shard_map/nd,sdf->snf/dot_general | solution.py:173
  475.5 26.5 %all-gather.11.cloned.1.call-done = bf16[1408,2048]{1,0:T(8,128)(2,1)} async-done(((bf16[1408,256]{1,0:T(8,128)(2,1)}), bf16[1408,2048]{1,0:T(8,128)(2,1)}) %all-gather.11.cloned.1.call-update) | async-done | bytes 5767184 | tf_op jit(solution)/shard_map/all_gather | solution.py:108
  502.0 15.6 fusion.71
  520.2 17.0 convolution_bitcast_fusion.4
  537.2 11.3 convolution_convert_fusion
  548.5 279.7 %all-reduce.7.cloned.1.call-done = f32[1024,2048]{1,0:T(8,128)} async-done(((f32[1024,2048]{1,0:T(8,128)}), f32[1024,2048]{1,0:T(8,128)}) %all-reduce.7.cloned.1.call-update) | async-done | bytes 8388624 | tf_op jit(solution)/shard_map/psum | solution.py:206
  846.1 130.8 %while.29 = (s32[]{:T(128)}, f32[1024,1,64]{0,2,1:T(8,128)}, f32[1024,1,64]{0,2,1:T(8,128)}, f32[2,512,1,8,64]{1,0,4,3,2:T(2,128)}, s32[2]{0:T(128)S(1)}, /*inde...) while((s32[]{:T(128)}, f32[1024,1,64]{0,2,1:T(8,128)}, ...), condition=%wide.region_14.15_spmd.clone, body=%wide.region_12.14_spmd.clone.sunk | while | flops 2728129024 | bytes 178747856 | solution.py:242
  855.6 10.8 fusion.181
  878.5 19.5 %dynamic_update_slice.22 = f32[2,512,1,8,64]{1,0,4,3,2:T(2,128)} dynamic-update-slice(f32[2,512,1,8,64]{1,0,4,3,2:T(2,128)} %get-tuple-element.553, f32[1,512,1,8,64]{1,0,4,3,2:T(1,128)S(1)} %copy.99, s32[]{:T(128)} %get-tuple-element.550, s32[]{:T(128)} %constant.54.clone.1..sunk.1, s32[]{:T(128)} %constant.54.clone.1..sunk.1, s32[]{:T(128)} %constant.54.clone.1..sunk.1, s32[]{:T(128)} %constant.54.clone.1..sunk.1) | dynamic-update-slice | bytes 2097156 | tf_op jit(solution)/shard_map/while/body/jit(dynamic_update_index_in_dim)/dynamic_update_slice | solution.py:242
  943.9 19.5 %dynamic_update_slice.22 = f32[2,512,1,8,64]{1,0,4,3,2:T(2,128)} dynamic-update-slice(f32[2,512,1,8,64]{1,0,4,3,2:T(2,128)} %get-tuple-element.553, f32[1,512,1,8,64]{1,0,4,3,2:T(1,128)S(1)} %copy.99, s32[]{:T(128)} %get-tuple-element.550, s32[]{:T(128)} %constant.54.clone.1..sunk.1, s32[]{:T(128)} %constant.54.clone.1..sunk.1, s32[]{:T(128)} %constant.54.clone.1..sunk.1, s32[]{:T(128)} %constant.54.clone.1..sunk.1) | dynamic-update-slice | bytes 2097156 | tf_op jit(solution)/shard_map/while/body/jit(dynamic_update_index_in_dim)/dynamic_update_slice | solution.py:242
  1013.0 269.4 %all-reduce.9.cloned.1.call-done = (bf16[1024,2048]{1,0:T(8,128)(2,1)}, bf16[1024,2048]{1,0:T(8,128)(2,1)}) async-done(((bf16[1024,2048]{1,0:T(8,128)(2,1)}, bf16[1024,2048]{1,0:T(8,128)(2,1)}), (bf16[1024,2048]{1,0:T(8,128)(2,1)}, bf16[1024,2048]{1,0:T(8,128)(2,1)})) %all-reduce.9.cloned.1.call-update) | async-done | bytes 8388624 | tf_op jit(solution)/shard_map/psum | solution.py:177
  1288.9 11.3 fusion.124
  1300.9 21.0 %convolution_bitcast_fusion.2 = f32[2,2048,1408]{1,2,0:T(8,128)} fusion(bf16[1,1024,1408]{2,1,0:T(8,128)(2,1)} %copy-done.57, bf16[1,1024,1408]{2,1,0:T(8,128)(2,1)} %copy-done.56, f32[1024,2048]{1,0:T(8,128)} %get-tuple-element.339, f32[2048]{0:T(1024)S(1)} %bitcast.367, f32[1024]{0:T(1024)S(1)} %copy-done.47), kind=kOutput, calls=%fused_computation.61 | convolution fusion | flops 11820335104 | bytes 37236736 | tf_op jit(solution)/shard_map/nd,snf->sdf/dot_general | solution.py:200
  1334.4 41.6 %reduce-scatter.9.cloned.1.call-done = f32[256,512]{1,0:T(8,128)} async-done(((f32[2048,512]{1,0:T(8,128)}), f32[256,512]{1,0:T(8,128)}) %reduce-scatter.9.cloned.1.call-update) | async-done | bytes 524304 | tf_op jit(solution)/shard_map/reduce_scatter | solution.py:268
  1379.0 51.8 %reduce-scatter.13.cloned.1.call-done = f32[512,256]{1,0:T(8,128)} async-done(((f32[512,2048]{1,0:T(8,128)}), f32[512,256]{1,0:T(8,128)}) %reduce-scatter.13.cloned.1.call-update) | async-done | bytes 524304 | tf_op jit(solution)/shard_map/reduce_scatter | solution.py:270
  1433.3 37.4 %reduce-scatter.19.cloned.1.call-done = f32[256,2]{1,0:T(8,128)} async-done(((f32[2048,2]{1,0:T(8,128)}), f32[256,2]{1,0:T(8,128)}) %reduce-scatter.19.cloned.1.call-update) | async-done | bytes 2064
  1472.9 87.9 %reduce-scatter.17.cloned.1.call-done = f32[1408,256]{1,0:T(8,128)} async-done(((f32[1408,2048]{1,0:T(8,128)}), f32[1408,256]{1,0:T(8,128)}) %reduce-scatter.17.cloned.1.call-update) | async-done | bytes 1441808 | tf_op jit(solution)/shard_map/reduce_scatter | solution.py:272
  1563.2 147.2 %reduce-scatter.15.cloned.1.call-done = f32[2,256,1408]{1,2,0:T(8,128)} async-done(((f32[2,2048,1408]{1,2,0:T(8,128)}), f32[2,256,1408]{1,2,0:T(8,128)}) %reduce-scatter.15.cloned.1.call-update) | async-done | bytes 2883600 | tf_op jit(solution)/shard_map/reduce_scatter | solution.py:271
  1724.3 12.2 psum.46
  1744.8 12.7 psum.47
  (285 shorter events, 289.3 us)
Async XLA Ops:
  7.2 18.8 %copy-start.33 = (f32[2,256,64]{1,2,0:T(8,128)S(1)}, f32[2,256,64]{1,2,0:T(8,128)}, u32[]{:S(2)}) copy-start(f32[2,256,64]{1,2,0:T(8,128)} %param.36) | copy-start | bytes 393220
  7.2 37.8 %all-gather.5.cloned.1.call-start = ((), (), s32[]{:S(2)}) async-start(), calls=%async_computation.6 | async-start | bytes 2359296 | tf_op jit(solution)/shard_map/all_gather | solution.py:104
  9.1 77.9 %all-gather.7.cloned.1.call-start = ((), (), s32[]{:S(2)}) async-start(), calls=%async_computation.7 | async-start | bytes 2359296 | tf_op jit(solution)/shard_map/all_gather | solution.py:106
  10.9 375.3 %all-reduce.5.cloned.1.call-start = ((), (), s32[]{:S(2)}) async-start(), calls=%async_computation.8 | async-start | bytes 16777216 | tf_op jit(solution)/shard_map/psum | solution.py:168
  11.0 29.2 %copy-start.2 = (bf16[1024,2048]{1,0:T(8,128)(2,1)S(1)}, bf16[1024,2048]{1,0:T(8,128)(2,1)}, u32[]{:S(2)}) copy-start(bf16[1024,2048]{1,0:T(8,128)(2,1)} %param.26) | copy-start | bytes 12582916
  22.9 22.1 %copy-start.42 = (f32[1,2048]{1,0:T(1,128)}, f32[1,2048]{1,0:T(1,128)S(1)}, u32[]{:S(2)}) copy-start(f32[1,2048]{1,0:T(1,128)S(1)} %get-tuple-element.356) | copy-start | bytes 24580
  26.0 19.0 %copy-start.48 = (f32[1024]{0:T(1024)}, f32[1024]{0:T(1024)S(1)}, u32[]{:S(2)}) copy-start(f32[1024]{0:T(1024)S(1)} %add_rsqrt_fusion.1) | copy-start | bytes 12292
  94.8 360.5 %all-gather.9.cloned.1.call-start = ((), (), s32[]{:S(2)}) async-start(), calls=%async_computation.9 | async-start | bytes 12976128 | tf_op jit(solution)/shard_map/all_gather | solution.py:107
  98.0 404.0 %all-gather.11.cloned.1.call-start = ((), (), s32[]{:S(2)}) async-start(), calls=%async_computation.10 | async-start | bytes 6488064 | tf_op jit(solution)/shard_map/all_gather | solution.py:108
  99.0 356.3 %copy-start.44 = (f32[1,2048]{1,0:T(1,128)S(1)}, f32[1,2048]{1,0:T(1,128)}, u32[]{:S(2)}) copy-start(f32[1,2048]{1,0:T(1,128)} %get-tuple-element.355) | copy-start | bytes 24580
  99.1 729.1 %all-reduce.7.cloned.1.call-start = ((), (), s32[]{:S(2)}) async-start(), calls=%async_computation.11 | async-start | bytes 16777216 | tf_op jit(solution)/shard_map/psum | solution.py:206
  395.5 440.3 %copy-start.46 = (f32[1024]{0:T(1024)}, f32[1024]{0:T(1024)S(1)}, u32[]{:S(2)}) copy-start(f32[1024]{0:T(1024)S(1)} %add_rsqrt_fusion) | copy-start | bytes 12292
  537.2 745.2 %all-reduce.9.cloned.1.call-start = ((), (), s32[]{:S(2)}) async-start(), calls=%async_computation.18 | async-start | bytes 16777216 | tf_op jit(solution)/shard_map/psum | solution.py:177
  828.2 9.4 copy-start.16
  877.4 20.6 %copy-start.7 = (f32[1024,1,64]{0,2,1:T(8,128)S(1)}, f32[1024,1,64]{0,2,1:T(8,128)}, u32[]{:S(2)}) copy-start(f32[1024,1,64]{0,2,1:T(8,128)} %get-tuple-element.551) | copy-start | bytes 786436 | tf_op jit(solution)/shard_map/while
  903.2 8.3 copy-start.4
  942.8 20.6 %copy-start.7 = (f32[1024,1,64]{0,2,1:T(8,128)S(1)}, f32[1024,1,64]{0,2,1:T(8,128)}, u32[]{:S(2)}) copy-start(f32[1024,1,64]{0,2,1:T(8,128)} %get-tuple-element.551) | copy-start | bytes 786436 | tf_op jit(solution)/shard_map/while
  968.6 8.3 copy-start.4
  991.7 341.1 %reduce-scatter.11.cloned.1.call-start = ((), (), s32[]{:S(2)}) async-start(), calls=%async_computation.13 | async-start | bytes 1179648 | tf_op jit(solution)/shard_map/reduce_scatter | solution.py:269
  997.0 379.0 %reduce-scatter.9.cloned.1.call-start = ((), (), s32[]{:S(2)}) async-start(), calls=%async_computation.12 | async-start | bytes 4718592 | tf_op jit(solution)/shard_map/reduce_scatter | solution.py:268
  1003.9 426.9 %reduce-scatter.13.cloned.1.call-start = ((), (), s32[]{:S(2)}) async-start(), calls=%async_computation.14 | async-start | bytes 4718592 | tf_op jit(solution)/shard_map/reduce_scatter | solution.py:270
  1013.0 457.7 %reduce-scatter.19.cloned.1.call-start = ((), (), s32[]{:S(2)}) async-start(), calls=%async_computation.17 | async-start | bytes 1179648
  1288.8 272.0 %reduce-scatter.17.cloned.1.call-start = ((), (), s32[]{:S(2)}) async-start(), calls=%async_computation.16 | async-start | bytes 12976128 | tf_op jit(solution)/shard_map/reduce_scatter | solution.py:272
  1300.2 410.2 %reduce-scatter.15.cloned.1.call-start = ((), (), s32[]{:S(2)}) async-start(), calls=%async_computation.15 | async-start | bytes 25952256 | tf_op jit(solution)/shard_map/reduce_scatter | solution.py:271
  (55 other events, 211.5 us)
Sparse Core Ops, SparseCore 0:
  10.5 32.9 all-gather.4
  45.9 28.5 all-gather.6
  94.9 291.2 all-reduce.4
  388.6 66.6 all-gather.8
  457.6 44.3 all-gather.10
  537.3 290.8 all-reduce.6
  991.8 290.5 all-reduce.8
  1286.2 35.0 reduce-scatter.10
  1324.6 51.3 reduce-scatter.8
  1379.5 51.2 reduce-scatter.12
  1434.6 36.0 reduce-scatter.18
  1474.0 86.7 reduce-scatter.16
  1564.4 145.9 reduce-scatter.14
